TPU v7x, 128 devices: a whole 4x4x4 slice. The times are simulated.
128 devices in a mesh: gx: 8 (over z, y_lo), gy: 16 (over x, y_hi, core).
Axes of the slice: x: 4, y: 4 (y_hi: 2, y_lo: 2; y = y_hi * 2 + y_lo), z: 4, core: 2. Of those that a mesh axis runs over, the one named last changes fastest.
Arguments:
- positions: float32 [3, 327680], P(None, ('gx', 'gy')), may hold values from 0 to 1
- velocities: float32 [3, 327680], P(None, ('gx', 'gy')), may hold values from -6 to 6
- block_order: int32 [128, 20], P(('gx', 'gy')), may hold values from 0 to 19, each once within a row
- flags: int32 [128, 20], P(('gx', 'gy')), may hold values from 0 to 1, as said below
- offsets: int32 [3, 3], replicated, may hold values from -1 to 1
- pixels: int32 [3, 327680], P(None, ('gx', 'gy')), may hold values from 0 to 1048575, as said below
Outputs:
- new_positions: float32 [3, 327680], P(None, ('gx', 'gy'))
- new_velocities: float32 [3, 327680], P(None, ('gx', 'gy'))
- maps: float32 [8192, 384], P(('gx', 'gy'))
Inputs may be any that keep to these rules, and one draw needn't show every extreme that they name: `flags`: each row holds 1 to 5 ones, and some row holds exactly 5. `block_order`: each row is a permutation. Among the 2560 columns of one slab cell and one replica, every strip of 8192 consecutive pixels is named exactly 2560 / 128 times.
All inputs are finite; a program needn't handle non-finite values.
Results may differ from a plain program's by a relative error of at most 0.0028.
Values may be sent and summed in bfloat16 or wider, within the bound.
A program may use at most 448 MiB of HBM per device.

v0:
```python
import jax
import jax.numpy as jnp
from jax import lax
from jax.sharding import PartitionSpec as P

MOVERS = 2
CROSS_MAX = 5
REPLICAS = 3
STRIP_ROWS = 64
time_step = 0.05
lane_count = 128


def passed_along(block, axis, distance):
    devices = range(lax.axis_size(axis))
    route = [((i - distance) % len(devices), i) for i in devices]
    return lax.ppermute(block, axis, route)


def sky_terms(shifted, speeds, live_mask):
    radius = jnp.sum(shifted * shifted, axis=1)
    weight = 1.0 / (1.0 + radius)
    radial = jnp.sum(speeds[None] * shifted, axis=1) / jnp.sqrt(1.0 + radius)
    energy = jnp.sum(speeds * speeds, axis=0) / 3.0
    return jnp.stack(
        [weight * live_mask, weight * radial * live_mask, weight * energy[None] * live_mask], axis=0
    ).astype(jnp.bfloat16)


def deposit(values, pixel_ids, target_of, row_total):
    entries = values.shape[0] * values.shape[2]
    flat_values = jnp.transpose(values, (0, 2, 1)).reshape(entries, 3)
    flat_ids = pixel_ids.reshape(entries)
    target = target_of(flat_ids // lane_count)
    lane_ids = flat_ids % lane_count
    row_hits = (target[None, :] == jnp.arange(row_total, dtype=jnp.int32)[:, None]).astype(
        jnp.bfloat16
    )
    lane_hits = (lane_ids[:, None] == jnp.arange(lane_count, dtype=jnp.int32)[None, :]).astype(
        jnp.bfloat16
    )
    spread = (flat_values[:, :, None] * lane_hits[:, None, :]).reshape(entries, 3 * lane_count)
    return jnp.dot(row_hits, spread, preferred_element_type=jnp.float32)


def on_device(positions, velocities, block_order, flags, offsets, pixels):
    blocks = block_order.shape[1]
    width = positions.shape[1] // blocks
    places = positions.reshape(3, blocks, width)
    speeds = velocities.reshape(3, blocks, width)
    places = places + time_step * speeds
    ordering = block_order[0]
    places = jnp.take(places, ordering, axis=1)
    speeds = jnp.take(speeds, ordering, axis=1)

    def leaving(which_set, component, sign_step):
        first_block = which_set * MOVERS
        moved_pos = places[:, first_block : first_block + MOVERS].at[component].add(sign_step)
        return (moved_pos, speeds[:, first_block : first_block + MOVERS])

    east_pos, east_vel = leaving(0, 0, -1.0)
    from_west = passed_along((east_pos, east_vel), "gx", 1)
    west_pos, west_vel = leaving(1, 0, 1.0)
    from_east = passed_along((west_pos, west_vel), "gx", -1)
    north_pos, north_vel = leaving(2, 1, -1.0)
    from_south = passed_along((north_pos, north_vel), "gy", 1)
    south_pos, south_vel = leaving(3, 1, 1.0)
    from_north = passed_along((south_pos, south_vel), "gy", -1)
    arrived = (from_west, from_east, from_south, from_north)
    new_places = jnp.concatenate(
        [places[:, 4 * MOVERS :]] + [received[0] for received in arrived], axis=1
    )
    new_speeds = jnp.concatenate(
        [speeds[:, 4 * MOVERS :]] + [received[1] for received in arrived], axis=1
    )
    count_x = lax.axis_size("gx")
    count_y = lax.axis_size("gy")
    cell_x = lax.axis_index("gx")
    cell_y = lax.axis_index("gy")
    owner_index = cell_x * count_y + cell_y
    flag_row = flags[0]
    ranking = (1 - flag_row) * blocks + jnp.arange(blocks, dtype=jnp.int32)
    chosen = jnp.argsort(ranking)[:CROSS_MAX]
    live_mask = jnp.take(flag_row, chosen).astype(jnp.float32).reshape(1, CROSS_MAX, 1)
    picked_pos = jnp.take(new_places, chosen, axis=1)
    picked_vel = jnp.take(new_speeds, chosen, axis=1)
    picked_ids = jnp.take(pixels.reshape(REPLICAS, blocks, width), chosen, axis=1)
    global_pos = jnp.stack(
        [
            (cell_x.astype(jnp.float32) + picked_pos[0]) / count_x,
            (cell_y.astype(jnp.float32) + picked_pos[1]) / count_y,
            picked_pos[2],
        ],
        axis=0,
    )
    shifted = global_pos[None] + offsets.astype(jnp.float32)[:, :, None, None]
    values = sky_terms(shifted, picked_vel, live_mask)
    send_values = jnp.transpose(values, (2, 0, 1, 3)).reshape(CROSS_MAX, 3, REPLICAS * width)
    send_ids = jnp.transpose(picked_ids, (1, 0, 2)).reshape(CROSS_MAX, REPLICAS * width)

    def in_strip(rows_global):
        return rows_global - owner_index * STRIP_ROWS

    maps = deposit(
        lax.all_gather(send_values, ("gx", "gy"), axis=0, tiled=True),
        lax.all_gather(send_ids, ("gx", "gy"), axis=0, tiled=True),
        in_strip,
        STRIP_ROWS,
    )
    return (new_places.reshape(3, blocks * width), new_speeds.reshape(3, blocks * width), maps)


def solution(mesh):
    in_specs = (
        P(None, ("gx", "gy")),
        P(None, ("gx", "gy")),
        P(("gx", "gy"), None),
        P(("gx", "gy"), None),
        P(),
        P(None, ("gx", "gy")),
    )
    out_specs = (P(None, ("gx", "gy")), P(None, ("gx", "gy")), P(("gx", "gy"), None))
    return jax.shard_map(
        on_device, mesh=mesh, in_specs=in_specs, out_specs=out_specs, check_vma=False
    )
```

profile of v0, /device:TPU:1, one launch (start us, length us, event | category | flops | bytes accessed | tf_op | source)
XLA Modules:
  0.0 567.8 jit_solution(4110377059390207661)
XLA Ops:
  7.2 0.0 copy-start
  7.2 0.0 all-gather.3.cloned.1.call-start
  7.2 0.7 compare_and_fusion
  7.9 0.7 compare_select_fusion
  8.6 0.8 bitcast_add_fusion
  9.4 1.4 gather_fusion.3
  10.7 0.6 gather_fusion.2
  11.3 0.1 select_bitcast_fusion
  11.4 1.5 collective-permute-start.7
  12.9 3.0 collective-permute-start.6
  15.9 4.5 collective-permute-start.5
  20.4 0.0 collective-permute-start.4
  20.4 0.9 collective-permute-start.2
  21.4 0.7 iota_add_fusion
  22.1 1.6 sort.17
  23.7 1.3 gather_fusion.1
  25.0 0.6 gather_fusion
  25.6 0.1 broadcast_select_fusion
  25.7 183.7 %all-gather = s32[128,5,384]{2,1,0:T(8,128)S(1)} all-gather(s32[1,5,384]{2,1,0:T(8,128)S(1)} %reshape.342), channel_id=1, replica_groups=mesh['gx'=8,'gy'=16] {'gx','gy'}, dimensions={0}, use_global_device_ids=true | all-gather | bytes 990720 | tf_op jit(solution)/shard_map/all_gather | solution.py:106
  209.4 0.2 reshape.286
  209.6 0.9 fusion.3
  210.4 0.7 convert_element_type.25
  211.2 0.0 collective-permute-done.4
  211.2 0.1 collective-permute-start
  211.3 0.0 collective-permute-done.5
  211.3 3.6 collective-permute-start.1
  214.9 0.0 collective-permute-done.6
  214.9 0.7 collective-permute-start.3
  215.6 0.0 collective-permute-done.7
  215.6 0.6 gather_fusion.5
  216.2 0.1 multiply_reduce_fusion
  216.3 0.0 collective-permute-done
  216.3 0.0 collective-permute-done.1
  216.4 0.0 collective-permute-done.2
  216.4 3.0 collective-permute-done.3
  219.4 0.6 gather_fusion.4
  220.0 0.1 select_bitcast_fusion.3
  220.1 0.1 fusion.7
  220.2 0.1 fusion.10
  220.3 0.6 reshape.287
  221.0 0.0 all-gather.3.cloned.1.call-update
  221.0 20.2 %fusion = bf16[245760,128]{0,1:T(8,128)(2,1)} fusion(s32[245760]{0:T(1024)S(1)} %get-tuple-element.62), kind=kLoop, calls=%fused_computation.7 | loop fusion | flops 62914560 | bytes 63897600 | tf_op jit(solution)/shard_map/convert_element_type | solution.py:39
  241.2 169.5 %all-gather.3.cloned.1.call-done = bf16[640,3,384]{2,1,0:T(4,128)(2,1)} async-done(((bf16[5,3,384]{2,1,0:T(4,128)(2,1)}), bf16[640,3,384]{2,1,0:T(4,128)(2,1)}) %all-gather.3.cloned.1.call-update) | async-done | bytes 1474576 | tf_op jit(solution)/shard_map/all_gather | solution.py:105
  410.7 81.4 %broadcast_multiply_fusion = bf16[245760,3,128]{0,2,1:T(8,128)(2,1)} fusion(bf16[245760,128]{0,1:T(8,128)(2,1)} %fusion, bf16[245760,3]{0,1:T(4,128)(2,1)} %bitcast.48), kind=kLoop, calls=%fused_computation.8 | loop fusion | flops 94371840 | bytes 253132800 | tf_op jit(solution)/shard_map/mul | solution.py:42
  492.1 0.0 copy-done.3
  492.2 0.0 copy-done.2
  492.2 0.0 copy-start.1
  492.2 68.8 %fusion.1 = f32[64,384]{1,0:T(8,128)} fusion(bf16[245760,384]{0,1:T(8,128)(2,1)} %bitcast.16, s32[245760]{0:T(1024)S(1)} %get-tuple-element.61), kind=kOutput, calls=%fused_computation.10 | convolution fusion | flops 12095324160 | bytes 189825024 | tf_op jit(solution)/shard_map/dot_general | solution.py:43
  (32 shorter events, 0.3 us)
Async XLA Ops:
  7.2 17.8 %copy-start = (s32[3,2560]{1,0:T(4,128)S(1)}, s32[3,2560]{1,0:T(4,128)}, u32[]{:S(2)}) copy-start(s32[3,2560]{1,0:T(4,128)} %param.23) | copy-start | bytes 92164
  7.2 403.5 %all-gather.3.cloned.1.call-start = ((), (), s32[]{:S(2)}) async-start(), calls=%async_computation | async-start | bytes 1981440 | tf_op jit(solution)/shard_map/all_gather | solution.py:105
  11.4 204.2 %collective-permute-start.7 = (f32[3,2,128]{2,0,1:T(4,128)S(1)}, f32[3,2,128]{2,0,1:T(4,128)S(1)}, u32[]{:S(2)}, u32[]{:S(2)}) collective-permute-start(f32[3,2,128]{2,0,1:T(4,128)S(1)} %get-tuple-element.63), channel_id=1, source_target_pairs={{1,0},{2,1},{3,2},{4,3},{5,4},{6,5},{7,6},{8,7},{9,8},{10,9},{11,1... | collective-permute-start | bytes 9224 | tf_op jit(solution)/shard_map/ppermute | solution.py:17
  12.9 201.9 %collective-permute-start.6 = (f32[3,2,128]{2,0,1:T(4,128)S(1)}, f32[3,2,128]{2,0,1:T(4,128)S(1)}, u32[]{:S(2)}, u32[]{:S(2)}) collective-permute-start(f32[3,2,128]{2,0,1:T(4,128)S(1)} %get-tuple-element.64), channel_id=1, source_target_pairs={{15,0},{0,1},{1,2},{2,3},{3,4},{4,5},{5,6},{6,7},{7,8},{8,9},{9,10... | collective-permute-start | bytes 9224 | tf_op jit(solution)/shard_map/ppermute | solution.py:17
  15.9 195.4 %collective-permute-start.5 = (f32[3,2,128]{2,0,1:T(4,128)S(1)}, f32[3,2,128]{2,0,1:T(4,128)S(1)}, u32[]{:S(2)}, u32[]{:S(2)}) collective-permute-start(f32[3,2,128]{2,0,1:T(4,128)S(1)} %get-tuple-element.65), channel_id=1, source_target_pairs={{16,0},{32,16},{48,32},{64,48},{80,64},{96,80},{112,96},{0,112},{1... | collective-permute-start | bytes 9224 | tf_op jit(solution)/shard_map/ppermute | solution.py:17
  20.4 190.9 %collective-permute-start.4 = (f32[3,2,128]{2,0,1:T(4,128)S(1)}, f32[3,2,128]{2,0,1:T(4,128)S(1)}, u32[]{:S(2)}, u32[]{:S(2)}) collective-permute-start(f32[3,2,128]{2,0,1:T(4,128)S(1)} %get-tuple-element.66), channel_id=1, source_target_pairs={{112,0},{0,16},{16,32},{32,48},{48,64},{64,80},{80,96},{96,112},{1... | collective-permute-start | bytes 9224 | tf_op jit(solution)/shard_map/ppermute | solution.py:17
  20.4 195.9 %collective-permute-start.2 = (f32[3,2,128]{2,0,1:T(4,128)S(1)}, f32[3,2,128]{2,0,1:T(4,128)S(1)}, u32[]{:S(2)}, u32[]{:S(2)}) collective-permute-start(f32[3,2,128]{2,0,1:T(4,128)S(1)} %scatter-add.16), channel_id=1, source_target_pairs={{15,0},{0,1},{1,2},{2,3},{3,4},{4,5},{5,6},{6,7},{7,8},{8,9},{9,10... | collective-permute-start | bytes 9224 | tf_op jit(solution)/shard_map/ppermute | solution.py:17
  211.2 5.1 collective-permute-start
  211.3 5.0 collective-permute-start.1
  214.9 4.5 collective-permute-start.3
  215.6 276.5 %copy-start.3 = (f32[3,20,128]{2,0,1:T(4,128)}, f32[3,20,128]{2,0,1:T(4,128)S(1)}, u32[]{:S(2)}) copy-start(f32[3,20,128]{2,0,1:T(4,128)S(1)} %constant_dynamic-update-slice_fusion.4) | copy-start | bytes 92164
  219.4 272.7 %copy-start.2 = (f32[3,20,128]{2,0,1:T(4,128)}, f32[3,20,128]{2,0,1:T(4,128)S(1)}, u32[]{:S(2)}) copy-start(f32[3,20,128]{2,0,1:T(4,128)S(1)} %constant_dynamic-update-slice_fusion) | copy-start | bytes 92164
  492.2 68.8 %copy-start.1 = (s32[3,2560]{1,0:T(4,128)S(1)}, s32[3,2560]{1,0:T(4,128)}, u32[]{:S(2)}) copy-start(s32[3,2560]{1,0:T(4,128)} %param.23) | copy-start | bytes 92164
Sparse Core Ops, SparseCore 0:
  221.1 189.5 all-gather.2
where the time goes:
time: 569 us; the launch traced here: 568 us
  blocking collectives  184 us (32%)
  waiting for transfers between devices  173 us (30%)
  other arithmetic  108 us (19%)
  matrix products  68.8 us (12%)
  starting transfers between devices  14.3 us (3%)
  between operations  14.3 us (3%)
  local copies, waits for them, and re-layouts  6.05 us (1%)
    all_gather x1, blocking collectives, on_device(): lax.all_gather(send_ids, ('gx', 'gy'), axis=0, tiled=True)  184 us
    all_gather x1, waiting for transfers between devices, on_device(): lax.all_gather(send_values, ('gx', 'gy'), axis=0, tiled=True)  170 us
    mul x1, other arithmetic, deposit(): flat_values[:, :, None] * lane_hits[:, None, :]  81.4 us
    dot_general x1, matrix products, deposit(): return jnp.dot(row_hits, spread, preferred_element_type=jnp.float32)  68.8 us
    convert_element_type x1, other arithmetic, deposit(): (lane_ids[:, None] == jnp.arange(lane_count, dtype=jnp.int32)[None, :]).a...  20.2 us
    ppermute x8, starting transfers between devices, passed_along(): return lax.ppermute(block, axis, route)  14.2 us
  transfers between devices with their start and end apart: 9, of which 2 were waited for; matrix products, arithmetic and copies ran while one was open for 5% of the time, Pallas kernels for 0%

commit v1 on v0

--- a/solution.py
+++ b/solution.py
@@ -103,7 +103,10 @@
 
     maps = deposit(
         lax.all_gather(send_values, ("gx", "gy"), axis=0, tiled=True),
-        lax.all_gather(send_ids, ("gx", "gy"), axis=0, tiled=True),
+        jnp.concatenate(
+            lax.all_to_all(jnp.stack([send_ids] * lax.axis_size(("gx", "gy"))), ("gx", "gy"), 0, 0),
+            axis=0,
+        ),
         in_strip,
         STRIP_ROWS,
     )

time: 569 us -> 419 us (0.74)
  blocking collectives: 184 us -> 0 us
  starting transfers between devices: 14.3 us -> 35.5 us
  waiting for transfers between devices: 173 us -> 185 us
    all_gather x1 -> x0, blocking collectives: 184 us -> none  [on_device(): lax.all_gather(send_ids, ('gx', 'gy'), axis=0, tiled=True)]
    all_to_all x0 -> x1, starting transfers between devices: none -> 11.7 us  [on_device(): lax.all_to_all(jnp.stack([send_ids] * lax.axis_size(('gx', 'gy'))), ('gx'...]
    ppermute x8, starting transfers between devices: 14.2 us -> 23.8 us  [passed_along(): return lax.ppermute(block, axis, route)]
    all_gather x1, waiting for transfers between devices: 170 us -> 176 us  [on_device(): lax.all_gather(send_values, ('gx', 'gy'), axis=0, tiled=True)]
  transfers between devices with their start and end apart: 9 -> 10, of which waited for: 2 -> 4; matrix products, arithmetic and copies ran while one was open for 5% -> 7% of each run, Pallas kernels for 0% -> 0%
where the time goes in v1:
time: 419 us
  waiting for transfers between devices  185 us (44%)
  other arithmetic  108 us (26%)
  matrix products  68.8 us (16%)
  starting transfers between devices  35.5 us (8%)
  between operations  14.3 us (3%)
  local copies, waits for them, and re-layouts  7.31 us (2%)
    all_gather x1, waiting for transfers between devices, on_device(): lax.all_gather(send_values, ('gx', 'gy'), axis=0, tiled=True)  176 us
    mul x1, other arithmetic, deposit(): flat_values[:, :, None] * lane_hits[:, None, :]  81.4 us
    dot_general x1, matrix products, deposit(): return jnp.dot(row_hits, spread, preferred_element_type=jnp.float32)  68.8 us
    ppermute x8, starting transfers between devices, passed_along(): return lax.ppermute(block, axis, route)  23.8 us
    convert_element_type x1, other arithmetic, deposit(): (lane_ids[:, None] == jnp.arange(lane_count, dtype=jnp.int32)[None, :]).a...  20.1 us
    all_to_all x1, starting transfers between devices, on_device(): lax.all_to_all(jnp.stack([send_ids] * lax.axis_size(('gx', 'gy'))), ('gx'...  11.7 us
    ppermute x8, waiting for transfers between devices, passed_along(): return lax.ppermute(block, axis, route)  8.53 us
  transfers between devices with their start and end apart: 10, of which 4 were waited for; matrix products, arithmetic and copies ran while one was open for 7% of the time, Pallas kernels for 0%

profile of v1, /device:TPU:1, one launch (start us, length us, event | category | flops | bytes accessed | tf_op | source)
XLA Modules:
  0.0 418.6 jit_solution(8564426414978760230)
XLA Ops:
  7.2 0.0 copy-start
  7.2 0.7 compare_and_fusion
  7.9 0.7 compare_select_fusion
  8.5 0.8 bitcast_add_fusion
  9.3 1.4 gather_fusion.3
  10.7 0.6 gather_fusion.2
  11.3 0.1 select_bitcast_fusion
  11.4 1.5 collective-permute-start.7
  12.9 3.0 collective-permute-start.6
  15.9 4.5 %collective-permute-start.5 = (f32[3,2,128]{2,0,1:T(4,128)S(1)}, f32[3,2,128]{2,0,1:T(4,128)S(1)}, u32[]{:S(2)}, u32[]{:S(2)}) collective-permute-start(f32[3,2,128]{2,0,1:T(4,128)S(1)} %get-tuple-element.65), channel_id=1, source_target_pairs={{16,0},{32,16},{48,32},{64,48},{80,64},{96,80},{112,96},{0,112},{1... | collective-permute-start | bytes 9224 | tf_op jit(solution)/shard_map/ppermute | solution.py:17
  20.3 0.0 collective-permute-start.4
  20.4 0.1 collective-permute-start
  20.5 0.7 iota_add_fusion
  21.1 1.6 sort.17
  22.8 0.6 gather_fusion
  23.3 0.1 select_bitcast_fusion.4
  23.4 1.3 stack.7
  24.7 11.7 %all-to-all-start = ((s32[128,5,384]{2,1,0:T(8,128)}), s32[128,5,384]{2,1,0:T(8,128)S(1)}, u32[]{:S(2)}, u32[]{:S(2)}) async-start(s32[128,5,384]{2,1,0:T(8,128)} %stack.7), calls=%async_computation | async-start | bytes 3145728 | tf_op jit(solution)/shard_map/all_to_all | solution.py:107
  36.4 0.0 all-gather.2.cloned.1.call-start
  36.5 1.3 gather_fusion.1
  37.8 0.7 convert_element_type.25
  38.6 0.0 collective-permute-done
  38.6 4.3 %collective-permute-start.1 = (f32[3,2,128]{2,0,1:T(4,128)S(1)}, f32[3,2,128]{2,0,1:T(4,128)S(1)}, u32[]{:S(2)}, u32[]{:S(2)}) collective-permute-start(f32[3,2,128]{2,0,1:T(4,128)S(1)} %scatter-add.15), channel_id=1, source_target_pairs={{16,0},{32,16},{48,32},{64,48},{80,64},{96,80},{112,96},{0,112},{1... | collective-permute-start | bytes 9224 | tf_op jit(solution)/shard_map/ppermute | solution.py:17
  42.9 7.0 %collective-permute-done.1 = f32[3,2,128]{2,0,1:T(4,128)S(1)} collective-permute-done((f32[3,2,128]{2,0,1:T(4,128)S(1)}, f32[3,2,128]{2,0,1:T(4,128)S(1)}, u32[]{:S(2)}, u32[]{:S(2)}) %collective-permute-start.1) | collective-permute-done | bytes 3104 | tf_op jit(solution)/shard_map/ppermute | solution.py:17
  49.9 4.5 %collective-permute-start.2 = (f32[3,2,128]{2,0,1:T(4,128)S(1)}, f32[3,2,128]{2,0,1:T(4,128)S(1)}, u32[]{:S(2)}, u32[]{:S(2)}) collective-permute-start(f32[3,2,128]{2,0,1:T(4,128)S(1)} %scatter-add.16), channel_id=1, source_target_pairs={{15,0},{0,1},{1,2},{2,3},{3,4},{4,5},{5,6},{6,7},{7,8},{8,9},{9,10... | collective-permute-start | bytes 9224 | tf_op jit(solution)/shard_map/ppermute | solution.py:17
  54.3 0.7 collective-permute-done.2
  55.1 6.0 %collective-permute-start.3 = (f32[3,2,128]{2,0,1:T(4,128)S(1)}, f32[3,2,128]{2,0,1:T(4,128)S(1)}, u32[]{:S(2)}, u32[]{:S(2)}) collective-permute-start(f32[3,2,128]{2,0,1:T(4,128)S(1)} %scatter-add.19), channel_id=1, source_target_pairs={{1,0},{2,1},{3,2},{4,3},{5,4},{6,5},{7,6},{8,7},{9,8},{10,9},{11,1... | collective-permute-start | bytes 9224 | tf_op jit(solution)/shard_map/ppermute | solution.py:17
  61.1 0.8 collective-permute-done.3
  61.9 0.6 gather_fusion.4
  62.5 0.1 select_bitcast_fusion.3
  62.6 0.0 collective-permute-done.4
  62.6 0.0 collective-permute-done.5
  62.6 0.0 collective-permute-done.6
  62.7 0.0 collective-permute-done.7
  62.7 0.0 copy-start.2
  62.7 0.6 gather_fusion.5
  63.3 0.1 multiply_reduce_fusion
  63.4 0.1 fusion.7
  63.5 0.1 fusion.10
  63.6 0.6 reshape.281
  64.2 0.0 all-gather.2.cloned.1.call-update
  64.2 0.2 reshape_reshape.3
  64.4 0.9 fusion.3
  65.3 20.1 %fusion = bf16[245760,128]{0,1:T(8,128)(2,1)} fusion(s32[245760]{0:T(1024)S(1)} %get-tuple-element.62), kind=kLoop, calls=%fused_computation.7 | loop fusion | flops 62914560 | bytes 63897600 | tf_op jit(solution)/shard_map/convert_element_type | solution.py:39
  85.4 176.0 %all-gather.2.cloned.1.call-done = bf16[640,3,384]{2,1,0:T(4,128)(2,1)} async-done(((bf16[5,3,384]{2,1,0:T(4,128)(2,1)}), bf16[640,3,384]{2,1,0:T(4,128)(2,1)}) %all-gather.2.cloned.1.call-update) | async-done | bytes 1474576 | tf_op jit(solution)/shard_map/all_gather | solution.py:105
  261.4 81.4 %broadcast_multiply_fusion = bf16[245760,3,128]{0,2,1:T(8,128)(2,1)} fusion(bf16[245760,128]{0,1:T(8,128)(2,1)} %fusion, bf16[245760,3]{0,1:T(4,128)(2,1)} %bitcast.53), kind=kLoop, calls=%fused_computation.8 | loop fusion | flops 94371840 | bytes 253132800 | tf_op jit(solution)/shard_map/mul | solution.py:42
  342.9 0.0 copy-start.1
  342.9 68.8 %fusion.1 = f32[64,384]{1,0:T(8,128)} fusion(bf16[245760,384]{0,1:T(8,128)(2,1)} %bitcast.16, s32[245760]{0:T(1024)S(1)} %get-tuple-element.61), kind=kOutput, calls=%fused_computation.10 | convolution fusion | flops 12095324160 | bytes 189825024 | tf_op jit(solution)/shard_map/dot_general | solution.py:43
  (33 shorter events, 0.3 us)
Async XLA Ops:
  7.2 15.6 %copy-start = (s32[3,2560]{1,0:T(4,128)S(1)}, s32[3,2560]{1,0:T(4,128)}, u32[]{:S(2)}) copy-start(s32[3,2560]{1,0:T(4,128)} %param.23) | copy-start | bytes 92164
  11.4 51.3 %collective-permute-start.7 = (f32[3,2,128]{2,0,1:T(4,128)S(1)}, f32[3,2,128]{2,0,1:T(4,128)S(1)}, u32[]{:S(2)}, u32[]{:S(2)}) collective-permute-start(f32[3,2,128]{2,0,1:T(4,128)S(1)} %get-tuple-element.63), channel_id=1, source_target_pairs={{1,0},{2,1},{3,2},{4,3},{5,4},{6,5},{7,6},{8,7},{9,8},{10,9},{11,1... | collective-permute-start | bytes 9224 | tf_op jit(solution)/shard_map/ppermute | solution.py:17
  12.9 49.7 %collective-permute-start.6 = (f32[3,2,128]{2,0,1:T(4,128)S(1)}, f32[3,2,128]{2,0,1:T(4,128)S(1)}, u32[]{:S(2)}, u32[]{:S(2)}) collective-permute-start(f32[3,2,128]{2,0,1:T(4,128)S(1)} %get-tuple-element.64), channel_id=1, source_target_pairs={{15,0},{0,1},{1,2},{2,3},{3,4},{4,5},{5,6},{6,7},{7,8},{8,9},{9,10... | collective-permute-start | bytes 9224 | tf_op jit(solution)/shard_map/ppermute | solution.py:17
  15.9 46.7 %collective-permute-start.5 = (f32[3,2,128]{2,0,1:T(4,128)S(1)}, f32[3,2,128]{2,0,1:T(4,128)S(1)}, u32[]{:S(2)}, u32[]{:S(2)}) collective-permute-start(f32[3,2,128]{2,0,1:T(4,128)S(1)} %get-tuple-element.65), channel_id=1, source_target_pairs={{16,0},{32,16},{48,32},{64,48},{80,64},{96,80},{112,96},{0,112},{1... | collective-permute-start | bytes 9224 | tf_op jit(solution)/shard_map/ppermute | solution.py:17
  20.3 42.3 %collective-permute-start.4 = (f32[3,2,128]{2,0,1:T(4,128)S(1)}, f32[3,2,128]{2,0,1:T(4,128)S(1)}, u32[]{:S(2)}, u32[]{:S(2)}) collective-permute-start(f32[3,2,128]{2,0,1:T(4,128)S(1)} %get-tuple-element.66), channel_id=1, source_target_pairs={{112,0},{0,16},{16,32},{32,48},{48,64},{64,80},{80,96},{96,112},{1... | collective-permute-start | bytes 9224 | tf_op jit(solution)/shard_map/ppermute | solution.py:17
  20.4 18.2 %collective-permute-start = (f32[3,2,128]{2,0,1:T(4,128)S(1)}, f32[3,2,128]{2,0,1:T(4,128)S(1)}, u32[]{:S(2)}, u32[]{:S(2)}) collective-permute-start(f32[3,2,128]{2,0,1:T(4,128)S(1)} %scatter-add.14), channel_id=1, source_target_pairs={{112,0},{0,16},{16,32},{32,48},{48,64},{64,80},{80,96},{96,112},{1... | collective-permute-start | bytes 9224 | tf_op jit(solution)/shard_map/ppermute | solution.py:17
  24.7 39.6 %all-to-all-start = ((s32[128,5,384]{2,1,0:T(8,128)}), s32[128,5,384]{2,1,0:T(8,128)S(1)}, u32[]{:S(2)}, u32[]{:S(2)}) async-start(s32[128,5,384]{2,1,0:T(8,128)} %stack.7), calls=%async_computation | async-start | bytes 3145728 | tf_op jit(solution)/shard_map/all_to_all | solution.py:107
  36.4 225.0 %all-gather.2.cloned.1.call-start = ((), (), s32[]{:S(2)}) async-start(), calls=%async_computation.1 | async-start | bytes 1981440 | tf_op jit(solution)/shard_map/all_gather | solution.py:105
  38.6 11.3 %collective-permute-start.1 = (f32[3,2,128]{2,0,1:T(4,128)S(1)}, f32[3,2,128]{2,0,1:T(4,128)S(1)}, u32[]{:S(2)}, u32[]{:S(2)}) collective-permute-start(f32[3,2,128]{2,0,1:T(4,128)S(1)} %scatter-add.15), channel_id=1, source_target_pairs={{16,0},{32,16},{48,32},{64,48},{80,64},{96,80},{112,96},{0,112},{1... | collective-permute-start | bytes 9224 | tf_op jit(solution)/shard_map/ppermute | solution.py:17
  49.9 5.2 %collective-permute-start.2 = (f32[3,2,128]{2,0,1:T(4,128)S(1)}, f32[3,2,128]{2,0,1:T(4,128)S(1)}, u32[]{:S(2)}, u32[]{:S(2)}) collective-permute-start(f32[3,2,128]{2,0,1:T(4,128)S(1)} %scatter-add.16), channel_id=1, source_target_pairs={{15,0},{0,1},{1,2},{2,3},{3,4},{4,5},{5,6},{6,7},{7,8},{8,9},{9,10... | collective-permute-start | bytes 9224 | tf_op jit(solution)/shard_map/ppermute | solution.py:17
  55.1 6.8 %collective-permute-start.3 = (f32[3,2,128]{2,0,1:T(4,128)S(1)}, f32[3,2,128]{2,0,1:T(4,128)S(1)}, u32[]{:S(2)}, u32[]{:S(2)}) collective-permute-start(f32[3,2,128]{2,0,1:T(4,128)S(1)} %scatter-add.19), channel_id=1, source_target_pairs={{1,0},{2,1},{3,2},{4,3},{5,4},{6,5},{7,6},{8,7},{9,8},{10,9},{11,1... | collective-permute-start | bytes 9224 | tf_op jit(solution)/shard_map/ppermute | solution.py:17
  61.9 280.9 %copy-start.3 = (f32[3,20,128]{2,0,1:T(4,128)}, f32[3,20,128]{2,0,1:T(4,128)S(1)}, u32[]{:S(2)}) copy-start(f32[3,20,128]{2,0,1:T(4,128)S(1)} %constant_dynamic-update-slice_fusion) | copy-start | bytes 92164
  62.7 280.2 %copy-start.2 = (f32[3,20,128]{2,0,1:T(4,128)}, f32[3,20,128]{2,0,1:T(4,128)S(1)}, u32[]{:S(2)}) copy-start(f32[3,20,128]{2,0,1:T(4,128)S(1)} %constant_dynamic-update-slice_fusion.4) | copy-start | bytes 92164
  342.9 68.8 %copy-start.1 = (s32[3,2560]{1,0:T(4,128)S(1)}, s32[3,2560]{1,0:T(4,128)}, u32[]{:S(2)}) copy-start(s32[3,2560]{1,0:T(4,128)} %param.23) | copy-start | bytes 92164
Sparse Core Ops, SparseCore 0:
  64.4 197.0 all-gather.1
